TPU v7x, 32 devices: a whole 2x2x4 slice. The times are simulated.
32 devices in a mesh: freq: 4 (over x, core), rows: 8 (over z, y).
Axes of the slice: x: 2, y: 2, z: 4, core: 2. Of those that a mesh axis runs over, the one named last changes fastest.
Arguments:
- time_loads: float32 [256, 192, 2048], P('freq', None, 'rows'), may hold values from -6 to 6
- factor: float32 [16, 2, 2048, 2048], P('freq', None, 'rows'), may hold values from -0.09375 to 0.09375
- diag_inverse: float32 [16, 2, 2048, 256], P('freq', None, 'rows'), may hold values from -0.25 to 0.25
- pivot_order: int32 [8], replicated, may hold values from 0 to 7, each once
Outputs:
- solution: float32 [16, 2, 192, 2048], P('freq', None, None, 'rows')
Inputs may be any that keep to these rules, and one draw needn't show every extreme that they name: `pivot_order`: a permutation of the 8 row blocks.
All inputs are finite; a program needn't handle non-finite values.
Results may differ from a plain program's by a relative error of at most 0.0001.
Values sent between devices are 32-bit elements; how exact they have to be, the bound alone decides.
A program may use at most 128 MiB of HBM per device.

v0:
```python
import jax
import jax.numpy as jnp
from jax import lax
from jax.sharding import PartitionSpec as P

FREQS = 16
STEPS = 256


def broadcast(value, axis, source):
    kept = jnp.where(lax.axis_index(axis) == source, value, 0).astype(value.dtype)
    return lax.psum(kept, axis)


def tables(count, length):
    freq_range = jnp.arange(count, dtype=jnp.float32)
    step_range = jnp.arange(length, dtype=jnp.float32)
    angles = 2.0 * jnp.pi * (freq_range[:, None] * step_range[None, :] % length) / length
    damping = jnp.exp(step_range * (jnp.log(0.1) / length))
    return (jnp.cos(angles) * damping[None, :], -jnp.sin(angles) * damping[None, :])


def product(matrix, vector):
    return jnp.einsum("fab,fcb->fca", matrix, vector, precision=lax.Precision.HIGHEST)


def complex_apply(matrix, vector):
    matrix_real, matrix_imag = (matrix[:, 0], matrix[:, 1])
    vector_real, vector_imag = (vector[:, 0], vector[:, 1])
    real_part = product(matrix_real, vector_real) - product(matrix_imag, vector_imag)
    imag_part = product(matrix_real, vector_imag) + product(matrix_imag, vector_real)
    return jnp.stack([real_part, imag_part], axis=1)


def body(time_loads, factor, diag_inverse, pivot_order):
    cosine_table, sine_table = tables(FREQS, STEPS)
    local_freqs = factor.shape[0]
    local_steps = time_loads.shape[0]
    offset = lax.axis_index("freq") * local_steps
    cosine_part = lax.dynamic_slice(
        cosine_table, (0, offset), (local_freqs * lax.axis_size("freq"), local_steps)
    )
    sine_part = lax.dynamic_slice(
        sine_table, (0, offset), (local_freqs * lax.axis_size("freq"), local_steps)
    )
    spectra = lax.psum_scatter(
        jnp.stack(
            [
                jnp.einsum("fn,ncr->fcr", cosine_part, time_loads, precision=lax.Precision.HIGHEST),
                jnp.einsum("fn,ncr->fcr", sine_part, time_loads, precision=lax.Precision.HIGHEST),
            ],
            axis=1,
        ),
        "freq",
        scatter_dimension=0,
        tiled=True,
    )
    my_block = lax.axis_index("rows")
    blocks = lax.axis_size("rows")
    block_rows = diag_inverse.shape[3]

    def advance(turn, state_pair):
        residual, solution = state_pair
        pivot_index = pivot_order[turn]
        is_owner = pivot_index == my_block
        solved = lax.cond(
            is_owner,
            lambda current: complex_apply(diag_inverse, current),
            lambda current: jnp.zeros_like(current),
            residual,
        )
        pivot = broadcast(solved, "rows", pivot_index)
        solution = jnp.where(is_owner, pivot, solution)
        column = lax.dynamic_slice_in_dim(factor, pivot_index * block_rows, block_rows, 3)
        residual = residual - complex_apply(column, pivot)
        return (residual, solution)

    residual, solution = lax.fori_loop(0, blocks, advance, (spectra, jnp.zeros_like(spectra)))
    return solution


def solution(mesh):
    placed = (
        P("freq", None, "rows"),
        P("freq", None, "rows", None),
        P("freq", None, "rows", None),
        P(),
    )
    return jax.shard_map(
        body, mesh=mesh, in_specs=placed, out_specs=P("freq", None, None, "rows"), check_vma=False
    )
```

profile of v0, /device:TPU:0, one launch (start us, length us, event | category | flops | bytes accessed | tf_op | source)
XLA Modules:
  0.0 998.1 jit_solution(14267200974558507674)
XLA Ops:
  6.7 18.0 %fusion.32 = f32[16,1,192,256]{3,0,2,1:T(8,128)S(1)} fusion(f32[64,192,256]{2,1,0:T(8,128)} %param.8, f32[16,256]{1,0:T(8,128)S(1)} %fusion.38, s32[]{:T(128)S(6)} %select_n.73, f32[64]{0:T(128)S(1)} %dynamic-slice.2), kind=kOutput, calls=%fused_computation.45 | convolution fusion | flops 603980800 | bytes 15737348 | tf_op jit(solution)/shard_map/fn,ncr->fcr/dot_general | solution.py:49
  24.6 13.5 %fusion.35 = f32[16,1,192,256]{3,0,2,1:T(8,128)S(1)} fusion(f32[64,192,256]{2,1,0:T(8,128)S(1)} %copy-done.4, f32[16,256]{1,0:T(8,128)S(1)} %fusion.38, s32[]{:T(128)S(6)} %select_n.73, f32[64]{0:T(128)S(1)} %dynamic-slice.2), kind=kOutput, calls=%fused_computation.46 | convolution fusion | flops 603981824 | bytes 15737348 | tf_op jit(solution)/shard_map/fn,ncr->fcr/dot_general | solution.py:50
  38.9 6.3 copy.13
  48.3 58.6 %reduce-scatter.2.cloned.1.call-done = f32[4,2,192,256]{3,2,1,0:T(8,128)} async-done(((f32[16,2,192,256]{3,2,1,0:T(8,128)}), f32[4,2,192,256]{3,2,1,0:T(8,128)}) %reduce-scatter.2.cloned.1.call-update) | async-done | bytes 1572880 | tf_op jit(solution)/shard_map/reduce_scatter | solution.py:46
  108.5 880.4 %while.18 = (s32[]{:T(128)}, f32[4,2,192,256]{3,2,0,1:T(8,128)S(1)}, f32[4,2,192,256]{3,2,0,1:T(8,128)}, s32[8]{0:T(128)S(1)}, s32[]{:T(128)}, /*index=5*/f32[4,...) while((s32[]{:T(128)}, ...), condition=%wide.region_5.6_spmd.clone, body=%wide.region_1.5_spmd.clone.sunk | while | flops 4835377152 | bytes 76546488 | solution.py:78
  112.5 93.3 %all-reduce.2.cloned.1.call-done = f32[4,2,192,256]{3,2,0,1:T(8,128)} async-done(((f32[4,2,192,256]{3,2,0,1:T(8,128)}), f32[4,2,192,256]{3,2,0,1:T(8,128)}) %all-reduce.2.cloned.1.call-update) | async-done | bytes 1572880 | tf_op jit(solution)/shard_map/while/body/eval_jaxpr/psum | solution.py:12
  205.8 2.8 fusion.61
  213.6 2.6 fusion.60
  222.4 93.2 %all-reduce.2.cloned.1.call-done = f32[4,2,192,256]{3,2,0,1:T(8,128)} async-done(((f32[4,2,192,256]{3,2,0,1:T(8,128)}), f32[4,2,192,256]{3,2,0,1:T(8,128)}) %all-reduce.2.cloned.1.call-update) | async-done | bytes 1572880 | tf_op jit(solution)/shard_map/while/body/eval_jaxpr/psum | solution.py:12
  315.6 2.8 fusion.61
  330.1 6.5 conditional.3
  338.5 86.0 %all-reduce.2.cloned.1.call-done = f32[4,2,192,256]{3,2,0,1:T(8,128)} async-done(((f32[4,2,192,256]{3,2,0,1:T(8,128)}), f32[4,2,192,256]{3,2,0,1:T(8,128)}) %all-reduce.2.cloned.1.call-update) | async-done | bytes 1572880 | tf_op jit(solution)/shard_map/while/body/eval_jaxpr/psum | solution.py:12
  424.5 2.8 fusion.61
  441.1 94.4 %all-reduce.2.cloned.1.call-done = f32[4,2,192,256]{3,2,0,1:T(8,128)} async-done(((f32[4,2,192,256]{3,2,0,1:T(8,128)}), f32[4,2,192,256]{3,2,0,1:T(8,128)}) %all-reduce.2.cloned.1.call-update) | async-done | bytes 1572880 | tf_op jit(solution)/shard_map/while/body/eval_jaxpr/psum | solution.py:12
  535.5 2.8 fusion.61
  552.1 93.5 %all-reduce.2.cloned.1.call-done = f32[4,2,192,256]{3,2,0,1:T(8,128)} async-done(((f32[4,2,192,256]{3,2,0,1:T(8,128)}), f32[4,2,192,256]{3,2,0,1:T(8,128)}) %all-reduce.2.cloned.1.call-update) | async-done | bytes 1572880 | tf_op jit(solution)/shard_map/while/body/eval_jaxpr/psum | solution.py:12
  645.5 2.8 fusion.61
  662.1 93.1 %all-reduce.2.cloned.1.call-done = f32[4,2,192,256]{3,2,0,1:T(8,128)} async-done(((f32[4,2,192,256]{3,2,0,1:T(8,128)}), f32[4,2,192,256]{3,2,0,1:T(8,128)}) %all-reduce.2.cloned.1.call-update) | async-done | bytes 1572880 | tf_op jit(solution)/shard_map/while/body/eval_jaxpr/psum | solution.py:12
  755.2 2.8 fusion.61
  771.8 93.5 %all-reduce.2.cloned.1.call-done = f32[4,2,192,256]{3,2,0,1:T(8,128)} async-done(((f32[4,2,192,256]{3,2,0,1:T(8,128)}), f32[4,2,192,256]{3,2,0,1:T(8,128)}) %all-reduce.2.cloned.1.call-update) | async-done | bytes 1572880 | tf_op jit(solution)/shard_map/while/body/eval_jaxpr/psum | solution.py:12
  865.3 2.8 fusion.61
  881.9 94.4 %all-reduce.2.cloned.1.call-done = f32[4,2,192,256]{3,2,0,1:T(8,128)} async-done(((f32[4,2,192,256]{3,2,0,1:T(8,128)}), f32[4,2,192,256]{3,2,0,1:T(8,128)}) %all-reduce.2.cloned.1.call-update) | async-done | bytes 1572880 | tf_op jit(solution)/shard_map/while/body/eval_jaxpr/psum | solution.py:12
  976.2 2.8 fusion.61
  988.9 2.7 copy.17
  (147 shorter events, 104.7 us)
Async XLA Ops:
  6.5 100.4 %reduce-scatter.2.cloned.1.call-start = ((), (), s32[]{:S(2)}) async-start(), calls=%async_computation.1 | async-start | bytes 7864320 | tf_op jit(solution)/shard_map/reduce_scatter | solution.py:46
  6.7 18.0 %copy-start.4 = (f32[64,192,256]{2,1,0:T(8,128)S(1)}, f32[64,192,256]{2,1,0:T(8,128)}, u32[]{:S(2)}) copy-start(f32[64,192,256]{2,1,0:T(8,128)} %param.8) | copy-start | bytes 37748740
  48.3 60.2 %copy-start.6 = (s32[8]{0:T(128)S(1)}, s32[8]{0:T(128)}, u32[]{:S(2)}) copy-start(s32[8]{0:T(128)} %param.11) | copy-start | bytes 100
  108.5 97.3 %all-reduce.2.cloned.1.call-start = ((), (), s32[]{:S(2)}) async-start(), calls=%async_computation.2 | async-start | bytes 3145728 | tf_op jit(solution)/shard_map/while/body/eval_jaxpr/psum | solution.py:12
  205.8 2.8 copy-start
  213.6 2.6 copy-start.2
  218.4 97.2 %all-reduce.2.cloned.1.call-start = ((), (), s32[]{:S(2)}) async-start(), calls=%async_computation.2 | async-start | bytes 3145728 | tf_op jit(solution)/shard_map/while/body/eval_jaxpr/psum | solution.py:12
  315.6 2.8 copy-start
  323.4 2.6 copy-start.2
  328.2 96.3 %all-reduce.2.cloned.1.call-start = ((), (), s32[]{:S(2)}) async-start(), calls=%async_computation.2 | async-start | bytes 3145728 | tf_op jit(solution)/shard_map/while/body/eval_jaxpr/psum | solution.py:12
  424.5 2.8 copy-start
  432.4 2.6 copy-start.2
  437.2 98.3 %all-reduce.2.cloned.1.call-start = ((), (), s32[]{:S(2)}) async-start(), calls=%async_computation.2 | async-start | bytes 3145728 | tf_op jit(solution)/shard_map/while/body/eval_jaxpr/psum | solution.py:12
  535.5 2.8 copy-start
  543.3 2.6 copy-start.2
  548.1 97.4 %all-reduce.2.cloned.1.call-start = ((), (), s32[]{:S(2)}) async-start(), calls=%async_computation.2 | async-start | bytes 3145728 | tf_op jit(solution)/shard_map/while/body/eval_jaxpr/psum | solution.py:12
  645.5 2.8 copy-start
  658.2 97.0 %all-reduce.2.cloned.1.call-start = ((), (), s32[]{:S(2)}) async-start(), calls=%async_computation.2 | async-start | bytes 3145728 | tf_op jit(solution)/shard_map/while/body/eval_jaxpr/psum | solution.py:12
  755.2 2.8 copy-start
  763.1 2.6 copy-start.2
  767.9 97.4 %all-reduce.2.cloned.1.call-start = ((), (), s32[]{:S(2)}) async-start(), calls=%async_computation.2 | async-start | bytes 3145728 | tf_op jit(solution)/shard_map/while/body/eval_jaxpr/psum | solution.py:12
  865.3 2.8 copy-start
  877.9 98.3 %all-reduce.2.cloned.1.call-start = ((), (), s32[]{:S(2)}) async-start(), calls=%async_computation.2 | async-start | bytes 3145728 | tf_op jit(solution)/shard_map/while/body/eval_jaxpr/psum | solution.py:12
  976.2 2.8 copy-start
  (13 other events, 21.6 us)
Sparse Core Ops, SparseCore 0:
  45.3 61.5 reduce-scatter.1
  112.8 92.8 all-reduce.1
  222.7 92.8 all-reduce.1
  338.0 86.4 all-reduce.1
  441.2 94.2 all-reduce.1
  552.1 93.3 all-reduce.1
  662.5 92.6 all-reduce.1
  772.2 93.0 all-reduce.1
  882.2 93.9 all-reduce.1
where the time goes:
time: 999 us; the launch traced here: 998 us
  waiting for transfers between devices  800 us (80%)
  matrix products  121 us (12%)
  local copies, waits for them, and re-layouts  29.1 us (3%)
  other arithmetic  19.2 us (2%)
  loops' own time  15.6 us (2%)
  between operations  13.1 us (1%)
    psum x8, waiting for transfers between devices, broadcast(): return lax.psum(kept, axis)  741 us
    dot_general x36, matrix products, product(): jnp.einsum('fab,fcb->fca', matrix, vector, precision=lax.Precision.HIGHEST)  89.5 us
    reduce_scatter x1, waiting for transfers between devices, body(): lax.psum_scatter(jnp.stack([jnp.einsum('fn,ncr->fcr', cosine_part, time_l...  58.6 us
  transfers between devices with their start and end apart: 9, of which 9 were waited for; matrix products, arithmetic and copies ran while one was open for 0% of the time, Pallas kernels for 0%

commit v1 on v0

--- a/solution.py
+++ b/solution.py
@@ -9,7 +9,7 @@
 
 def broadcast(value, axis, source):
     kept = jnp.where(lax.axis_index(axis) == source, value, 0).astype(value.dtype)
-    return lax.psum(kept, axis)
+    return jnp.sum(lax.all_gather(kept, axis), axis=0)
 
 
 def tables(count, length):

time: 999 us -> 1730 us (1.73)
  waiting for transfers between devices: 800 us -> 1490 us
  other arithmetic: 19.2 us -> 64 us
    all_gather x0 -> x8, waiting for transfers between devices: none -> 1430 us  [broadcast(): return jnp.sum(lax.all_gather(kept, axis), axis=0)]
    psum x8 -> x0, waiting for transfers between devices: 741 us -> none  [broadcast(): return lax.psum(kept, axis)]
    reduce_sum x0 -> x8, other arithmetic: none -> 44.9 us  [broadcast(): return jnp.sum(lax.all_gather(kept, axis), axis=0)]
where the time goes in v1:
time: 1730 us
  waiting for transfers between devices  1490 us (86%)
  matrix products  118 us (7%)
  other arithmetic  64 us (4%)
  local copies, waits for them, and re-layouts  28.3 us (2%)
    all_gather x8, waiting for transfers between devices, broadcast(): return jnp.sum(lax.all_gather(kept, axis), axis=0)  1430 us
    dot_general x36, matrix products, product(): jnp.einsum('fab,fcb->fca', matrix, vector, precision=lax.Precision.HIGHEST)  86.7 us
    reduce_scatter x1, waiting for transfers between devices, body(): lax.psum_scatter(jnp.stack([jnp.einsum('fn,ncr->fcr', cosine_part, time_l...  58.6 us
    reduce_sum x8, other arithmetic, broadcast(): return jnp.sum(lax.all_gather(kept, axis), axis=0)  44.9 us
  transfers between devices with their start and end apart: 9, of which 9 were waited for; matrix products, arithmetic and copies ran while one was open for 0% of the time, Pallas kernels for 0%

profile of v1, /device:TPU:0, one launch (start us, length us, event | category | flops | bytes accessed | tf_op | source)
XLA Modules:
  0.0 1727.7 jit_solution(16391901214046768033)
XLA Ops:
  6.7 18.0 %fusion.32 = f32[16,1,192,256]{3,0,2,1:T(8,128)S(1)} fusion(f32[64,192,256]{2,1,0:T(8,128)} %param.8, f32[16,256]{1,0:T(8,128)S(1)} %fusion.38, s32[]{:T(128)S(6)} %select_n.73, f32[64]{0:T(128)S(1)} %dynamic-slice.2), kind=kOutput, calls=%fused_computation.45 | convolution fusion | flops 603980800 | bytes 15737348 | tf_op jit(solution)/shard_map/fn,ncr->fcr/dot_general | solution.py:49
  24.6 13.5 fusion.35
  38.9 6.3 copy.13
  48.3 58.6 %reduce-scatter.2.cloned.1.call-done = f32[4,2,192,256]{3,2,1,0:T(8,128)} async-done(((f32[16,2,192,256]{3,2,1,0:T(8,128)}), f32[4,2,192,256]{3,2,1,0:T(8,128)}) %reduce-scatter.2.cloned.1.call-update) | async-done | bytes 1572880 | tf_op jit(solution)/shard_map/reduce_scatter | solution.py:46
  108.5 1610.0 %while.18 = (s32[]{:T(128)}, f32[4,2,192,256]{3,2,0,1:T(8,128)S(1)}, f32[4,2,192,256]{3,2,0,1:T(8,128)}, s32[8]{0:T(128)S(1)}, s32[]{:T(128)}, /*index=5*/f32[4,...) while((s32[]{:T(128)}, ...), condition=%wide.region_5.6_spmd.clone, body=%wide.region_1.5_spmd.clone.sunk | while | flops 4837736448 | bytes 117440944 | solution.py:78
  112.3 180.2 %all-gather.6.cloned.1.call-done = f32[32,2,192,256]{3,2,0,1:T(8,128)} async-done(((f32[4,2,192,256]{3,2,0,1:T(8,128)}), f32[32,2,192,256]{3,2,0,1:T(8,128)}) %all-gather.6.cloned.1.call-update) | async-done | bytes 12582928 | tf_op jit(solution)/shard_map/while/body/eval_jaxpr/all_gather | solution.py:12
  292.4 5.6 reduce_sum.18
  314.0 179.2 %all-gather.6.cloned.1.call-done = f32[32,2,192,256]{3,2,0,1:T(8,128)} async-done(((f32[4,2,192,256]{3,2,0,1:T(8,128)}), f32[32,2,192,256]{3,2,0,1:T(8,128)}) %all-gather.6.cloned.1.call-update) | async-done | bytes 12582928 | tf_op jit(solution)/shard_map/while/body/eval_jaxpr/all_gather | solution.py:12
  493.2 5.6 reduce_sum.18
  512.8 6.5 conditional.3
  512.8 2.6 fusion.6
  521.1 172.9 %all-gather.6.cloned.1.call-done = f32[32,2,192,256]{3,2,0,1:T(8,128)} async-done(((f32[4,2,192,256]{3,2,0,1:T(8,128)}), f32[32,2,192,256]{3,2,0,1:T(8,128)}) %all-gather.6.cloned.1.call-update) | async-done | bytes 12582928 | tf_op jit(solution)/shard_map/while/body/eval_jaxpr/all_gather | solution.py:12
  694.0 5.6 reduce_sum.18
  715.6 180.1 %all-gather.6.cloned.1.call-done = f32[32,2,192,256]{3,2,0,1:T(8,128)} async-done(((f32[4,2,192,256]{3,2,0,1:T(8,128)}), f32[32,2,192,256]{3,2,0,1:T(8,128)}) %all-gather.6.cloned.1.call-update) | async-done | bytes 12582928 | tf_op jit(solution)/shard_map/while/body/eval_jaxpr/all_gather | solution.py:12
  895.7 5.6 reduce_sum.18
  917.2 180.2 %all-gather.6.cloned.1.call-done = f32[32,2,192,256]{3,2,0,1:T(8,128)} async-done(((f32[4,2,192,256]{3,2,0,1:T(8,128)}), f32[32,2,192,256]{3,2,0,1:T(8,128)}) %all-gather.6.cloned.1.call-update) | async-done | bytes 12582928 | tf_op jit(solution)/shard_map/while/body/eval_jaxpr/all_gather | solution.py:12
  1097.4 5.6 reduce_sum.18
  1119.0 178.3 %all-gather.6.cloned.1.call-done = f32[32,2,192,256]{3,2,0,1:T(8,128)} async-done(((f32[4,2,192,256]{3,2,0,1:T(8,128)}), f32[32,2,192,256]{3,2,0,1:T(8,128)}) %all-gather.6.cloned.1.call-update) | async-done | bytes 12582928 | tf_op jit(solution)/shard_map/while/body/eval_jaxpr/all_gather | solution.py:12
  1297.3 5.6 reduce_sum.18
  1318.8 180.1 %all-gather.6.cloned.1.call-done = f32[32,2,192,256]{3,2,0,1:T(8,128)} async-done(((f32[4,2,192,256]{3,2,0,1:T(8,128)}), f32[32,2,192,256]{3,2,0,1:T(8,128)}) %all-gather.6.cloned.1.call-update) | async-done | bytes 12582928 | tf_op jit(solution)/shard_map/while/body/eval_jaxpr/all_gather | solution.py:12
  1498.9 5.6 reduce_sum.18
  1520.5 180.2 %all-gather.6.cloned.1.call-done = f32[32,2,192,256]{3,2,0,1:T(8,128)} async-done(((f32[4,2,192,256]{3,2,0,1:T(8,128)}), f32[32,2,192,256]{3,2,0,1:T(8,128)}) %all-gather.6.cloned.1.call-update) | async-done | bytes 12582928 | tf_op jit(solution)/shard_map/while/body/eval_jaxpr/all_gather | solution.py:12
  1700.7 5.6 reduce_sum.18
  1718.5 2.7 copy.17
  (139 shorter events, 123.8 us)
Async XLA Ops:
  6.5 100.4 %reduce-scatter.2.cloned.1.call-start = ((), (), s32[]{:S(2)}) async-start(), calls=%async_computation.1 | async-start | bytes 7864320 | tf_op jit(solution)/shard_map/reduce_scatter | solution.py:46
  6.7 18.0 %copy-start.3 = (f32[64,192,256]{2,1,0:T(8,128)S(1)}, f32[64,192,256]{2,1,0:T(8,128)}, u32[]{:S(2)}) copy-start(f32[64,192,256]{2,1,0:T(8,128)} %param.8) | copy-start | bytes 37748740
  45.2 1.6 copy-start.4
  48.3 60.2 %copy-start.5 = (s32[8]{0:T(128)S(1)}, s32[8]{0:T(128)}, u32[]{:S(2)}) copy-start(s32[8]{0:T(128)} %param.11) | copy-start | bytes 100
  108.5 183.9 %all-gather.6.cloned.1.call-start = ((), (), s32[]{:S(2)}) async-start(), calls=%async_computation.2 | async-start | bytes 14155776 | tf_op jit(solution)/shard_map/while/body/eval_jaxpr/all_gather | solution.py:12
  305.5 2.6 copy-start.1
  309.1 1.2 copy-start.2
  310.3 182.9 %all-gather.6.cloned.1.call-start = ((), (), s32[]{:S(2)}) async-start(), calls=%async_computation.2 | async-start | bytes 14155776 | tf_op jit(solution)/shard_map/while/body/eval_jaxpr/all_gather | solution.py:12
  506.3 2.6 copy-start.1
  509.9 1.2 copy-start.2
  511.1 182.9 %all-gather.6.cloned.1.call-start = ((), (), s32[]{:S(2)}) async-start(), calls=%async_computation.2 | async-start | bytes 14155776 | tf_op jit(solution)/shard_map/while/body/eval_jaxpr/all_gather | solution.py:12
  512.8 2.6 copy-start
  707.1 2.6 copy-start.1
  710.7 1.2 copy-start.2
  711.9 183.8 %all-gather.6.cloned.1.call-start = ((), (), s32[]{:S(2)}) async-start(), calls=%async_computation.2 | async-start | bytes 14155776 | tf_op jit(solution)/shard_map/while/body/eval_jaxpr/all_gather | solution.py:12
  908.7 2.6 copy-start.1
  913.5 183.9 %all-gather.6.cloned.1.call-start = ((), (), s32[]{:S(2)}) async-start(), calls=%async_computation.2 | async-start | bytes 14155776 | tf_op jit(solution)/shard_map/while/body/eval_jaxpr/all_gather | solution.py:12
  1110.5 2.6 copy-start.1
  1115.3 182.0 %all-gather.6.cloned.1.call-start = ((), (), s32[]{:S(2)}) async-start(), calls=%async_computation.2 | async-start | bytes 14155776 | tf_op jit(solution)/shard_map/while/body/eval_jaxpr/all_gather | solution.py:12
  1310.4 2.6 copy-start.1
  1315.1 183.8 %all-gather.6.cloned.1.call-start = ((), (), s32[]{:S(2)}) async-start(), calls=%async_computation.2 | async-start | bytes 14155776 | tf_op jit(solution)/shard_map/while/body/eval_jaxpr/all_gather | solution.py:12
  1512.0 2.6 copy-start.1
  1516.8 183.9 %all-gather.6.cloned.1.call-start = ((), (), s32[]{:S(2)}) async-start(), calls=%async_computation.2 | async-start | bytes 14155776 | tf_op jit(solution)/shard_map/while/body/eval_jaxpr/all_gather | solution.py:12
  1713.7 2.6 copy-start.1
  (5 other events, 5.8 us)
Sparse Core Ops, SparseCore 0:
  45.3 61.5 reduce-scatter.1
  111.8 180.5 all-gather.5
  313.6 179.6 all-gather.5
  520.7 173.3 all-gather.5
  715.2 180.4 all-gather.5
  916.8 180.5 all-gather.5
  1118.5 178.7 all-gather.5
  1318.4 180.4 all-gather.5
  1520.0 180.5 all-gather.5
